TPU v7x, 32 devices: a whole 2x2x4 slice. The times are simulated.
32 devices in a mesh: leaf: 4 (over z), row: 2 (over x), top: 4 (over y, core).
Axes of the slice: x: 2, y: 2, z: 4, core: 2. Of those that a mesh axis runs over, the one named last changes fastest.
Arguments:
- loads: bfloat16 [4, 2, 4, 1, 256, 32], P('leaf', 'row', 'top'), may hold values from -6 to 6
- flux_maps: bfloat16 [4, 2, 4, 640, 256], P('leaf', 'row', 'top'), may hold values from -0.375 to 0.375
- chain_maps: float32 [4, 2, 4, 640, 640], P('leaf', 'row', 'top')
- leaf_maps: bfloat16 [4, 2, 4, 1, 256, 256], P('leaf', 'row', 'top'), may hold values from -0.375 to 0.375
- edge_maps: bfloat16 [4, 2, 4, 1, 256, 640], P('leaf', 'row', 'top'), may hold values from -0.25 to 0.25
- top_maps: bfloat16 [4, 2, 4, 1, 256, 128], P('leaf', 'row', 'top'), may hold values from -0.5 to 0.5
- slot_nodes: int32 [4, 2, 4, 128], P('leaf', 'row', 'top'), may hold values from 0 to 8191
- slot_counts: int32 [4, 2, 4], P('leaf', 'row', 'top'), may hold values from 1 to 128, 320 in all within a row
- top_loads: float32 [8192, 32], P('leaf'), may hold values from -6 to 6
- top_inverse: float32 [8192, 8192], P('top', ('leaf', 'row')), may hold values from -0.0625 to 0.0625
Outputs:
- solution: bfloat16 [4, 2, 4, 1, 256, 32], P('leaf', 'row', 'top')
- top_values: float32 [8192, 32], P('top')
Inputs may be any that keep to these rules, and one draw needn't show every extreme that they name: `slot_counts`: over the 4 subtrees of one x-y cell (same x and y, all t) the live slots sum to 320, and one of those subtrees has all 128 slots live.
All inputs are finite; a program needn't handle non-finite values. No bound on the sum of `slot_counts` on one device may be relied on, other than what follows from the above.
Results may differ from a plain program's by a relative error of at most 0.0046.
Values sent between devices are 32-bit elements; how exact they have to be, the bound alone decides.
A program may use at most 64 MiB of HBM per device.

v0:
```python
import jax
import jax.numpy as jnp
from jax import lax
from jax.sharding import PartitionSpec as P


def passed_along(value, axis, steps):
    count = lax.axis_size(axis)
    first, last = (max(0, -steps), min(count, count - steps))
    return lax.ppermute(value, axis, [(source, source + steps) for source in range(first, last)])


def body(
    loads,
    flux_maps,
    chain_maps,
    leaf_maps,
    edge_maps,
    top_maps,
    slot_nodes,
    slot_counts,
    top_loads,
    top_inverse,
):
    leaf_count = loads.shape[3]
    node_count = loads.shape[4]
    rhs_count = loads.shape[5]
    sep_width = chain_maps.shape[-1]
    slot_total = slot_nodes.shape[-1]
    largest_level = lax.Precision.HIGHEST
    local_loads = loads.reshape(leaf_count, node_count, rhs_count)
    flattened = loads.reshape(leaf_count * node_count, rhs_count)
    fluxes = jnp.dot(
        flux_maps.reshape(sep_width, leaf_count * node_count),
        flattened,
        preferred_element_type=jnp.float32,
    )
    combine_operator = chain_maps.reshape(sep_width, sep_width)
    chain_index = lax.axis_index("leaf")

    def advance(step_index, carried):
        earlier = passed_along(carried, "leaf", 1)
        advanced = (
            jnp.dot(
                combine_operator,
                earlier,
                precision=largest_level,
                preferred_element_type=jnp.float32,
            )
            + fluxes
        )
        return jnp.where(chain_index == step_index, advanced, carried)

    states = lax.fori_loop(1, lax.axis_size("leaf"), advance, fluxes)
    slot_ids = slot_nodes.reshape(slot_total)
    is_live = lax.iota(jnp.int32, slot_total) < slot_counts.reshape(())
    chosen_entries = jnp.where(is_live[:, None], states[:slot_total], jnp.float32(0.0))
    block_rows = top_loads.shape[0]
    row_ids = lax.iota(jnp.int32, block_rows * lax.axis_size("leaf"))
    match_table = (row_ids[:, None] == slot_ids[None, :]).astype(jnp.float32)
    top_block = lax.psum_scatter(
        jnp.dot(
            match_table, chosen_entries, precision=largest_level, preferred_element_type=jnp.float32
        ),
        "leaf",
        scatter_dimension=0,
        tiled=True,
    )
    top_block = lax.psum(top_block, ("row", "top"))
    rhs_block = top_loads - top_block
    column_rows = top_inverse.shape[1]
    rhs_piece = lax.dynamic_slice_in_dim(
        rhs_block, lax.axis_index("row") * column_rows, column_rows, 0
    )
    partial_value = jnp.dot(
        top_inverse, rhs_piece, precision=largest_level, preferred_element_type=jnp.float32
    )
    owned_rows = lax.psum(partial_value, ("leaf", "row"))
    shard_piece = lax.all_gather(owned_rows, "top", axis=0, tiled=True)
    row_ids = lax.iota(jnp.int32, shard_piece.shape[0])
    match_table = ((slot_ids[:, None] == row_ids[None, :]) & is_live[:, None]).astype(jnp.float32)
    boundary = jnp.dot(
        match_table, shard_piece, precision=largest_level, preferred_element_type=jnp.float32
    )
    states_low = states.astype(jnp.bfloat16)
    boundary_low = boundary.astype(jnp.bfloat16)
    summed = jnp.einsum(
        "lij,ljr->lir",
        leaf_maps.reshape(leaf_count, node_count, node_count),
        local_loads,
        preferred_element_type=jnp.float32,
    )
    summed = summed + jnp.einsum(
        "lik,kr->lir",
        edge_maps.reshape(leaf_count, node_count, sep_width),
        states_low,
        preferred_element_type=jnp.float32,
    )
    summed = summed + jnp.einsum(
        "lic,cr->lir",
        top_maps.reshape(leaf_count, node_count, slot_total),
        boundary_low,
        preferred_element_type=jnp.float32,
    )
    solution = summed.astype(jnp.bfloat16).reshape(1, 1, 1, leaf_count, node_count, rhs_count)
    return (solution, owned_rows)


def solution(mesh):
    in_specs = (
        P("leaf", "row", "top", None, None, None),
        P("leaf", "row", "top", None, None),
        P("leaf", "row", "top", None, None),
        P("leaf", "row", "top", None, None, None),
        P("leaf", "row", "top", None, None, None),
        P("leaf", "row", "top", None, None, None),
        P("leaf", "row", "top", None),
        P("leaf", "row", "top"),
        P("leaf", None),
        P("top", ("leaf", "row")),
    )
    out_specs = (P("leaf", "row", "top", None, None, None), P("top", None))
    return jax.shard_map(body, mesh=mesh, in_specs=in_specs, out_specs=out_specs, check_vma=False)
```

profile of v0, /device:TPU:0, one launch (start us, length us, event | category | flops | bytes accessed | tf_op | source)
XLA Modules:
  0.0 237.6 jit_solution(16142841711911786712)
XLA Ops:
  7.2 0.0 reduce-scatter.2.cloned.1.call-start
  7.9 0.2 copy-done
  8.2 0.9 fusion.15
  9.1 29.0 %while.13 = (s32[]{:T(128)}, f32[640,32]{0,1:T(8,128)S(1)}, s32[]{:T(128)}, f32[640,640]{1,0:T(8,128)}, f32[640,32]{0,1:T(8,128)S(1)}, /*index=5*/s32[]{:T(128)}) while((s32[]{:T(128)}, f32[640,32]{0,1:T(8,128)S(1)}, s32[]{:T(128)}, f32[640,640]{1,0:T(8,128)}, f32[640,32]{0,1:T(8,128)S(1)}, /*index=5*/s32[]{:T(128)}) %tuple.44), condition=%wide.region_1.2_spmd, body=%wide.region_0.1_spmd.sunk | while | flops 157327360 | bytes 2293879 | solution.py:54
  9.1 5.1 %collective-permute-start = (f32[640,32]{0,1:T(8,128)S(1)}, f32[640,32]{0,1:T(8,128)S(1)}, u32[]{:S(2)}, u32[]{:S(2)}) collective-permute-start(f32[640,32]{0,1:T(8,128)S(1)} %get-tuple-element.145), channel_id=1, source_target_pairs={{0,8},{8,16},{16,24},{1,9},{9,17},{17,25},{2,10},{10,18},{18,26},{... | collective-permute-start | bytes 245768 | tf_op jit(solution)/shard_map/while/body/eval_jaxpr/ppermute | solution.py:10
  14.2 2.0 collective-permute-done
  16.3 3.1 %fusion.39 = f32[640,32]{0,1:T(8,128)S(1)} fusion(f32[640,32]{0,1:T(8,128)S(1)} %get-tuple-element.145, f32[640,32]{0,1:T(8,128)S(1)} %get-tuple-element.154, f32[640,640]{1,0:T(8,128)} %get-tuple-element.153, f32[640,32]{0,1:T(8,128)S(1)} %collective-permute-done, pred[]{:T(512)S(6)} %eq.69), kind=kOutput, calls=%fused_computation.1.clone.1 | convolution fusion | flops 157327360 | bytes 1966081 | tf_op jit(solution)/shard_map/while/body/eval_jaxpr/dot_general | solution.py:44
  19.4 4.3 %collective-permute-start = (f32[640,32]{0,1:T(8,128)S(1)}, f32[640,32]{0,1:T(8,128)S(1)}, u32[]{:S(2)}, u32[]{:S(2)}) collective-permute-start(f32[640,32]{0,1:T(8,128)S(1)} %get-tuple-element.145), channel_id=1, source_target_pairs={{0,8},{8,16},{16,24},{1,9},{9,17},{17,25},{2,10},{10,18},{18,26},{... | collective-permute-start | bytes 245768 | tf_op jit(solution)/shard_map/while/body/eval_jaxpr/ppermute | solution.py:10
  23.7 2.0 collective-permute-done
  25.7 3.1 %fusion.39 = f32[640,32]{0,1:T(8,128)S(1)} fusion(f32[640,32]{0,1:T(8,128)S(1)} %get-tuple-element.145, f32[640,32]{0,1:T(8,128)S(1)} %get-tuple-element.154, f32[640,640]{1,0:T(8,128)} %get-tuple-element.153, f32[640,32]{0,1:T(8,128)S(1)} %collective-permute-done, pred[]{:T(512)S(6)} %eq.69), kind=kOutput, calls=%fused_computation.1.clone.1 | convolution fusion | flops 157327360 | bytes 1966081 | tf_op jit(solution)/shard_map/while/body/eval_jaxpr/dot_general | solution.py:44
  28.8 4.3 %collective-permute-start = (f32[640,32]{0,1:T(8,128)S(1)}, f32[640,32]{0,1:T(8,128)S(1)}, u32[]{:S(2)}, u32[]{:S(2)}) collective-permute-start(f32[640,32]{0,1:T(8,128)S(1)} %get-tuple-element.145), channel_id=1, source_target_pairs={{0,8},{8,16},{16,24},{1,9},{9,17},{17,25},{2,10},{10,18},{18,26},{... | collective-permute-start | bytes 245768 | tf_op jit(solution)/shard_map/while/body/eval_jaxpr/ppermute | solution.py:10
  33.1 2.0 collective-permute-done
  35.1 3.1 %fusion.39 = f32[640,32]{0,1:T(8,128)S(1)} fusion(f32[640,32]{0,1:T(8,128)S(1)} %get-tuple-element.145, f32[640,32]{0,1:T(8,128)S(1)} %get-tuple-element.154, f32[640,640]{1,0:T(8,128)} %get-tuple-element.153, f32[640,32]{0,1:T(8,128)S(1)} %collective-permute-done, pred[]{:T(512)S(6)} %eq.69), kind=kOutput, calls=%fused_computation.1.clone.1 | convolution fusion | flops 157327360 | bytes 1966081 | tf_op jit(solution)/shard_map/while/body/eval_jaxpr/dot_general | solution.py:44
  38.2 3.3 %fusion.2 = f32[8192,32]{0,1:T(8,128)} fusion(s32[128]{0:T(128)S(1)} %bitcast.45, f32[640,32]{0,1:T(8,128)S(1)} %get-tuple-element.96, pred[128]{0:T(512)(128)(4,1)S(1)} %iota_compare_fusion.3), kind=kOutput, calls=%fused_computation.5 | convolution fusion | flops 403705856 | bytes 1065984 | tf_op jit(solution)/shard_map/dot_general | solution.py:62
  41.5 0.0 reduce-scatter.2.cloned.1.call-update
  41.5 0.0 all-reduce.3.cloned.1.call-start
  41.6 29.4 %reduce-scatter.2.cloned.1.call-done = f32[2048,32]{0,1:T(8,128)} async-done(((f32[8192,32]{0,1:T(8,128)}), f32[2048,32]{0,1:T(8,128)}) %reduce-scatter.2.cloned.1.call-update) | async-done | bytes 262160 | tf_op jit(solution)/shard_map/reduce_scatter | solution.py:61
  71.0 0.0 all-reduce.3.cloned.1.call-update
  71.0 0.0 all-reduce.5.cloned.1.call-start
  71.1 55.4 %all-reduce.3.cloned.1.call-done = f32[2048,32]{0,1:T(8,128)} async-done(((f32[2048,32]{0,1:T(8,128)}), f32[2048,32]{0,1:T(8,128)}) %all-reduce.3.cloned.1.call-update) | async-done | bytes 262160 | tf_op jit(solution)/shard_map/psum | solution.py:69
  126.5 11.7 %convolution_bitcast_fusion = f32[2048,32]{0,1:T(8,128)} fusion(f32[2048,1024]{1,0:T(8,128)} %param.21, f32[2048,32]{0,1:T(8,128)} %all-reduce.3.cloned.1.call-done, s32[]{:T(128)S(6)} %select_n.24, f32[2048,32]{0,1:T(8,128)S(1)} %copy-done.4), kind=kOutput, calls=%fused_computation.7 | convolution fusion | flops 805339136 | bytes 8912900 | tf_op jit(solution)/shard_map/dot_general | solution.py:75
  138.2 0.0 all-reduce.5.cloned.1.call-update
  138.2 0.0 all-gather.2.cloned.1.call-start
  138.2 70.5 %all-reduce.5.cloned.1.call-done = f32[2048,32]{0,1:T(8,128)} async-done(((f32[2048,32]{0,1:T(8,128)}), f32[2048,32]{0,1:T(8,128)}) %all-reduce.5.cloned.1.call-update) | async-done | bytes 262160 | tf_op jit(solution)/shard_map/psum | solution.py:78
  208.7 0.0 all-gather.2.cloned.1.call-update
  208.8 0.2 convolution_bitcast_fusion.2
  208.9 0.0 copy-done.3
  209.0 0.2 convolution_add_fusion.1
  209.2 16.9 %all-gather.2.cloned.1.call-done = f32[8192,32]{0,1:T(8,128)} async-done(((f32[2048,32]{0,1:T(8,128)}), f32[8192,32]{0,1:T(8,128)}) %all-gather.2.cloned.1.call-update) | async-done | bytes 1048592 | tf_op jit(solution)/shard_map/all_gather | solution.py:79
  226.1 3.5 %fusion.8 = bf16[128,32]{1,0:T(8,128)(2,1)S(1)} fusion(f32[8192,32]{0,1:T(8,128)} %all-gather.2.cloned.1.call-done, s32[128]{0:T(128)S(1)} %bitcast.46, pred[128]{0:T(512)(128)(4,1)S(1)} %iota_compare_fusion.3), kind=kOutput, calls=%fused_computation.11 | convolution fusion | flops 404754432 | bytes 1057408 | tf_op jit(solution)/shard_map/dot_general | solution.py:82
  229.6 0.8 fusion.13
  230.4 0.7 copy.21
  (16 shorter events, 0.1 us)
Async XLA Ops:
  7.2 1.0 copy-start
  7.2 63.8 %reduce-scatter.2.cloned.1.call-start = ((), (), s32[]{:S(2)}) async-start(), calls=%async_computation.1 | async-start | bytes 1310720 | tf_op jit(solution)/shard_map/reduce_scatter | solution.py:61
  9.1 29.1 %copy-start.7 = (s32[1,1,1,128]{3,2,1,0:T(1,128)S(1)}, s32[1,1,1,128]{3,2,1,0:T(1,128)}, u32[]{:S(2)}) copy-start(s32[1,1,1,128]{3,2,1,0:T(1,128)} %param.18) | copy-start | bytes 1540
  9.1 117.4 %copy-start.4 = (f32[2048,32]{0,1:T(8,128)S(1)}, f32[2048,32]{0,1:T(8,128)}, u32[]{:S(2)}) copy-start(f32[2048,32]{0,1:T(8,128)} %param.20) | copy-start | bytes 786436
  9.1 7.1 %collective-permute-start = (f32[640,32]{0,1:T(8,128)S(1)}, f32[640,32]{0,1:T(8,128)S(1)}, u32[]{:S(2)}, u32[]{:S(2)}) collective-permute-start(f32[640,32]{0,1:T(8,128)S(1)} %get-tuple-element.145), channel_id=1, source_target_pairs={{0,8},{8,16},{16,24},{1,9},{9,17},{17,25},{2,10},{10,18},{18,26},{... | collective-permute-start | bytes 245768 | tf_op jit(solution)/shard_map/while/body/eval_jaxpr/ppermute | solution.py:10
  19.4 6.3 %collective-permute-start = (f32[640,32]{0,1:T(8,128)S(1)}, f32[640,32]{0,1:T(8,128)S(1)}, u32[]{:S(2)}, u32[]{:S(2)}) collective-permute-start(f32[640,32]{0,1:T(8,128)S(1)} %get-tuple-element.145), channel_id=1, source_target_pairs={{0,8},{8,16},{16,24},{1,9},{9,17},{17,25},{2,10},{10,18},{18,26},{... | collective-permute-start | bytes 245768 | tf_op jit(solution)/shard_map/while/body/eval_jaxpr/ppermute | solution.py:10
  28.8 6.3 %collective-permute-start = (f32[640,32]{0,1:T(8,128)S(1)}, f32[640,32]{0,1:T(8,128)S(1)}, u32[]{:S(2)}, u32[]{:S(2)}) collective-permute-start(f32[640,32]{0,1:T(8,128)S(1)} %get-tuple-element.145), channel_id=1, source_target_pairs={{0,8},{8,16},{16,24},{1,9},{9,17},{17,25},{2,10},{10,18},{18,26},{... | collective-permute-start | bytes 245768 | tf_op jit(solution)/shard_map/while/body/eval_jaxpr/ppermute | solution.py:10
  41.5 84.9 %all-reduce.3.cloned.1.call-start = ((), (), s32[]{:S(2)}) async-start(), calls=%async_computation.2 | async-start | bytes 524288 | tf_op jit(solution)/shard_map/psum | solution.py:69
  71.0 137.7 %all-reduce.5.cloned.1.call-start = ((), (), s32[]{:S(2)}) async-start(), calls=%async_computation.3 | async-start | bytes 524288 | tf_op jit(solution)/shard_map/psum | solution.py:78
  71.1 137.7 %copy-start.2 = (bf16[1,1,1,1,256,640]{5,4,3,2,1,0:T(8,128)(2,1)S(1)}, bf16[1,1,1,1,256,640]{5,4,3,2,1,0:T(8,128)(2,1)}, u32[]{:S(2)}) copy-start(bf16[1,1,1,1,256,640]{5,4,3,2,1,0:T(8,128)(2,1)} %param.16) | copy-start | bytes 983044
  71.1 137.9 %copy-start.3 = (bf16[1,1,1,1,256,256]{5,4,3,2,1,0:T(8,128)(2,1)S(1)}, bf16[1,1,1,1,256,256]{5,4,3,2,1,0:T(8,128)(2,1)}, u32[]{:S(2)}) copy-start(bf16[1,1,1,1,256,256]{5,4,3,2,1,0:T(8,128)(2,1)} %param.15) | copy-start | bytes 393220
  71.1 137.9 %copy-start.6 = (bf16[1,1,1,1,256,32]{4,5,3,2,1,0:T(8,128)(2,1)S(1)}, bf16[1,1,1,1,256,32]{4,5,3,2,1,0:T(8,128)(2,1)}, u32[]{:S(2)}) copy-start(bf16[1,1,1,1,256,32]{4,5,3,2,1,0:T(8,128)(2,1)} %param.12) | copy-start | bytes 49156
  138.2 91.4 %copy-start.5 = (bf16[1,1,1,1,256,128]{5,4,3,2,1,0:T(8,128)(2,1)S(1)}, bf16[1,1,1,1,256,128]{5,4,3,2,1,0:T(8,128)(2,1)}, u32[]{:S(2)}) copy-start(bf16[1,1,1,1,256,128]{5,4,3,2,1,0:T(8,128)(2,1)} %param.17) | copy-start | bytes 196612
  138.2 87.9 %all-gather.2.cloned.1.call-start = ((), (), s32[]{:S(2)}) async-start(), calls=%async_computation.4 | async-start | bytes 1310720 | tf_op jit(solution)/shard_map/all_gather | solution.py:79
  208.7 21.6 %copy-start.1 = (f32[2048,32]{0,1:T(8,128)S(1)}, f32[2048,32]{0,1:T(8,128)}, u32[]{:S(2)}) copy-start(f32[2048,32]{0,1:T(8,128)} %all-reduce.5.cloned.1.call-done) | copy-start | bytes 786436
Sparse Core Ops, SparseCore 0:
  41.6 29.3 reduce-scatter.1
  74.1 52.3 all-reduce.2
  138.3 70.3 all-reduce.4
  210.2 15.8 all-gather.1
where the time goes:
time: 238 us
  waiting for transfers between devices  178 us (75%)
  matrix products  29.7 us (12%)
  between operations  14.6 us (6%)
  starting transfers between devices  13.8 us (6%)
    psum x1, waiting for transfers between devices, body(): owned_rows = lax.psum(partial_value, ('leaf', 'row'))  70.5 us
    psum x1, waiting for transfers between devices, body(): top_block = lax.psum(top_block, ('row', 'top'))  55.4 us
    reduce_scatter x1, waiting for transfers between devices, body(): lax.psum_scatter(jnp.dot(match_table, chosen_entries, precision=largest_l...  29.4 us
    all_gather x1, waiting for transfers between devices, body(): shard_piece = lax.all_gather(owned_rows, 'top', axis=0, tiled=True)  16.9 us
    ppermute x3, starting transfers between devices, passed_along(): lax.ppermute(value, axis, [(source, source + steps) for source in range(f...  13.7 us
    dot_general x1, matrix products, body(): jnp.dot(top_inverse, rhs_piece, precision=largest_level, preferred_elemen...  11.7 us
    dot_general x3, matrix products, advance(): jnp.dot(combine_operator, earlier, precision=largest_level, preferred_ele...  9.17 us
    ppermute x3, waiting for transfers between devices, passed_along(): lax.ppermute(value, axis, [(source, source + steps) for source in range(f...  6.09 us
  transfers between devices with their start and end apart: 7, of which 7 were waited for; matrix products, arithmetic and copies ran while one was open for 0% of the time, Pallas kernels for 0%

commit v1 on v0

--- a/solution.py
+++ b/solution.py
@@ -66,7 +66,7 @@
         scatter_dimension=0,
         tiled=True,
     )
-    top_block = lax.psum(top_block, ("row", "top"))
+    top_block = jnp.sum(jax.lax.all_gather(top_block, ("row", "top")), axis=0)
     rhs_block = top_loads - top_block
     column_rows = top_inverse.shape[1]
     rhs_piece = lax.dynamic_slice_in_dim(

time: 238 us -> 214 us (0.90)
  waiting for transfers between devices: 178 us -> 152 us
  local copies, waits for them, and re-layouts: 1.05 us -> 3.85 us
    psum x1 -> x0, waiting for transfers between devices: 55.4 us -> none  [body(): top_block = lax.psum(top_block, ('row', 'top'))]
    all_gather x0 -> x1, waiting for transfers between devices: none -> 28.1 us  [body(): top_block = jnp.sum(jax.lax.all_gather(top_block, ('row', 'top')), axis=0)]
    unnamed x18 -> x19, local copies, waits for them, and re-layouts: 1.05 us -> 3.85 us
where the time goes in v1:
time: 214 us; the launch traced here: 213 us
  waiting for transfers between devices  152 us (71%)
  matrix products  28.6 us (13%)
  between operations  14.6 us (7%)
  starting transfers between devices  13.7 us (6%)
  local copies, waits for them, and re-layouts  3.85 us (2%)
    psum x1, waiting for transfers between devices, body(): owned_rows = lax.psum(partial_value, ('leaf', 'row'))  71.1 us
    reduce_scatter x1, waiting for transfers between devices, body(): lax.psum_scatter(jnp.dot(match_table, chosen_entries, precision=largest_l...  29.5 us
    all_gather x1, waiting for transfers between devices, body(): top_block = jnp.sum(jax.lax.all_gather(top_block, ('row', 'top')), axis=0)  28.1 us
    all_gather x1, waiting for transfers between devices, body(): shard_piece = lax.all_gather(owned_rows, 'top', axis=0, tiled=True)  16.9 us
    ppermute x3, starting transfers between devices, passed_along(): lax.ppermute(value, axis, [(source, source + steps) for source in range(f...  13.5 us
    dot_general x1, matrix products, body(): jnp.dot(top_inverse, rhs_piece, precision=largest_level, preferred_elemen...  10.6 us
    dot_general x3, matrix products, advance(): jnp.dot(combine_operator, earlier, precision=largest_level, preferred_ele...  9.17 us
    ppermute x3, waiting for transfers between devices, passed_along(): lax.ppermute(value, axis, [(source, source + steps) for source in range(f...  6.09 us
  transfers between devices with their start and end apart: 7, of which 7 were waited for; matrix products, arithmetic and copies ran while one was open for 0% of the time, Pallas kernels for 0%

profile of v1, /device:TPU:0, one launch (start us, length us, event | category | flops | bytes accessed | tf_op | source)
XLA Modules:
  0.0 213.2 jit_solution(3093330935586319221)
XLA Ops:
  7.2 0.0 reduce-scatter.2.cloned.1.call-start
  7.9 0.2 copy-done
  8.2 0.9 fusion.15
  9.1 28.9 %while.13 = (s32[]{:T(128)}, f32[640,32]{0,1:T(8,128)S(1)}, s32[]{:T(128)}, f32[640,640]{1,0:T(8,128)}, f32[640,32]{0,1:T(8,128)S(1)}, /*index=5*/s32[]{:T(128)}) while((s32[]{:T(128)}, f32[640,32]{0,1:T(8,128)S(1)}, s32[]{:T(128)}, f32[640,640]{1,0:T(8,128)}, f32[640,32]{0,1:T(8,128)S(1)}, /*index=5*/s32[]{:T(128)}) %tuple.44), condition=%wide.region_1.2_spmd, body=%wide.region_0.1_spmd.sunk | while | flops 157327360 | bytes 2293879 | solution.py:54
  9.1 5.0 %collective-permute-start = (f32[640,32]{0,1:T(8,128)S(1)}, f32[640,32]{0,1:T(8,128)S(1)}, u32[]{:S(2)}, u32[]{:S(2)}) collective-permute-start(f32[640,32]{0,1:T(8,128)S(1)} %get-tuple-element.145), channel_id=1, source_target_pairs={{0,8},{8,16},{16,24},{1,9},{9,17},{17,25},{2,10},{10,18},{18,26},{... | collective-permute-start | bytes 245768 | tf_op jit(solution)/shard_map/while/body/eval_jaxpr/ppermute | solution.py:10
  14.1 2.0 collective-permute-done
  16.1 3.1 %fusion.39 = f32[640,32]{0,1:T(8,128)S(1)} fusion(f32[640,32]{0,1:T(8,128)S(1)} %get-tuple-element.145, f32[640,32]{0,1:T(8,128)S(1)} %get-tuple-element.154, f32[640,640]{1,0:T(8,128)} %get-tuple-element.153, f32[640,32]{0,1:T(8,128)S(1)} %collective-permute-done, pred[]{:T(512)S(6)} %eq.69), kind=kOutput, calls=%fused_computation.1.clone.1 | convolution fusion | flops 157327360 | bytes 1966081 | tf_op jit(solution)/shard_map/while/body/eval_jaxpr/dot_general | solution.py:44
  19.2 4.3 %collective-permute-start = (f32[640,32]{0,1:T(8,128)S(1)}, f32[640,32]{0,1:T(8,128)S(1)}, u32[]{:S(2)}, u32[]{:S(2)}) collective-permute-start(f32[640,32]{0,1:T(8,128)S(1)} %get-tuple-element.145), channel_id=1, source_target_pairs={{0,8},{8,16},{16,24},{1,9},{9,17},{17,25},{2,10},{10,18},{18,26},{... | collective-permute-start | bytes 245768 | tf_op jit(solution)/shard_map/while/body/eval_jaxpr/ppermute | solution.py:10
  23.5 2.0 collective-permute-done
  25.5 3.1 %fusion.39 = f32[640,32]{0,1:T(8,128)S(1)} fusion(f32[640,32]{0,1:T(8,128)S(1)} %get-tuple-element.145, f32[640,32]{0,1:T(8,128)S(1)} %get-tuple-element.154, f32[640,640]{1,0:T(8,128)} %get-tuple-element.153, f32[640,32]{0,1:T(8,128)S(1)} %collective-permute-done, pred[]{:T(512)S(6)} %eq.69), kind=kOutput, calls=%fused_computation.1.clone.1 | convolution fusion | flops 157327360 | bytes 1966081 | tf_op jit(solution)/shard_map/while/body/eval_jaxpr/dot_general | solution.py:44
  28.6 4.3 %collective-permute-start = (f32[640,32]{0,1:T(8,128)S(1)}, f32[640,32]{0,1:T(8,128)S(1)}, u32[]{:S(2)}, u32[]{:S(2)}) collective-permute-start(f32[640,32]{0,1:T(8,128)S(1)} %get-tuple-element.145), channel_id=1, source_target_pairs={{0,8},{8,16},{16,24},{1,9},{9,17},{17,25},{2,10},{10,18},{18,26},{... | collective-permute-start | bytes 245768 | tf_op jit(solution)/shard_map/while/body/eval_jaxpr/ppermute | solution.py:10
  32.9 2.0 collective-permute-done
  35.0 3.1 %fusion.39 = f32[640,32]{0,1:T(8,128)S(1)} fusion(f32[640,32]{0,1:T(8,128)S(1)} %get-tuple-element.145, f32[640,32]{0,1:T(8,128)S(1)} %get-tuple-element.154, f32[640,640]{1,0:T(8,128)} %get-tuple-element.153, f32[640,32]{0,1:T(8,128)S(1)} %collective-permute-done, pred[]{:T(512)S(6)} %eq.69), kind=kOutput, calls=%fused_computation.1.clone.1 | convolution fusion | flops 157327360 | bytes 1966081 | tf_op jit(solution)/shard_map/while/body/eval_jaxpr/dot_general | solution.py:44
  38.0 3.3 %fusion.2 = f32[8192,32]{0,1:T(8,128)} fusion(s32[128]{0:T(128)S(1)} %bitcast.51, f32[640,32]{0,1:T(8,128)S(1)} %get-tuple-element.96, pred[128]{0:T(512)(128)(4,1)S(1)} %iota_compare_fusion.3), kind=kOutput, calls=%fused_computation.5 | convolution fusion | flops 403705856 | bytes 1065984 | tf_op jit(solution)/shard_map/dot_general | solution.py:62
  41.3 0.0 reduce-scatter.2.cloned.1.call-update
  41.4 0.0 all-gather.6.cloned.1.call-start
  41.4 29.5 %reduce-scatter.2.cloned.1.call-done = f32[2048,32]{0,1:T(8,128)} async-done(((f32[8192,32]{0,1:T(8,128)}), f32[2048,32]{0,1:T(8,128)}) %reduce-scatter.2.cloned.1.call-update) | async-done | bytes 262160 | tf_op jit(solution)/shard_map/reduce_scatter | solution.py:61
  70.9 0.0 all-gather.6.cloned.1.call-update
  70.9 0.0 all-reduce.2.cloned.1.call-start
  71.0 28.1 %all-gather.6.cloned.1.call-done = f32[16384,32]{0,1:T(8,128)} async-done(((f32[2048,32]{0,1:T(8,128)}), f32[16384,32]{0,1:T(8,128)}) %all-gather.6.cloned.1.call-update) | async-done | bytes 2097168 | tf_op jit(solution)/shard_map/all_gather | solution.py:69
  99.1 2.8 %copy.12 = f32[4,8,8,2048]{3,2,1,0:T(8,128)S(1)} copy(f32[4,8,8,2048]{3,1,2,0:T(8,128)} %bitcast.50) | data formatting | bytes 4194304
  101.9 0.5 bitcast_reduce_fusion
  102.5 10.6 %convolution_bitcast_fusion = f32[2048,32]{0,1:T(8,128)} fusion(f32[2048,1024]{1,0:T(8,128)} %param.21, f32[2048,32]{0,1:T(8,128)S(1)} %bitcast_reduce_fusion, s32[]{:T(128)S(6)} %select_n.24, f32[2048,32]{0,1:T(8,128)S(1)} %copy-done.4), kind=kOutput, calls=%fused_computation.7 | convolution fusion | flops 805339136 | bytes 8912900 | tf_op jit(solution)/shard_map/dot_general | solution.py:75
  113.2 0.0 all-gather.4.cloned.1.call-start
  113.2 71.1 %all-reduce.2.cloned.1.call-done = f32[2048,32]{0,1:T(8,128)} async-done(((f32[2048,32]{0,1:T(8,128)}), f32[2048,32]{0,1:T(8,128)}) %all-reduce.2.cloned.1.call-update) | async-done | bytes 262160 | tf_op jit(solution)/shard_map/psum | solution.py:78
  184.4 0.2 convolution_bitcast_fusion.2
  184.5 0.0 copy-done.3
  184.6 0.2 convolution_add_fusion.1
  184.7 16.9 %all-gather.4.cloned.1.call-done = f32[8192,32]{0,1:T(8,128)} async-done(((f32[2048,32]{0,1:T(8,128)}), f32[8192,32]{0,1:T(8,128)}) %all-gather.4.cloned.1.call-update) | async-done | bytes 1048592 | tf_op jit(solution)/shard_map/all_gather | solution.py:79
  201.7 3.5 %fusion.8 = bf16[128,32]{1,0:T(8,128)(2,1)S(1)} fusion(f32[8192,32]{0,1:T(8,128)} %all-gather.4.cloned.1.call-done, s32[128]{0:T(128)S(1)} %bitcast.52, pred[128]{0:T(512)(128)(4,1)S(1)} %iota_compare_fusion.3), kind=kOutput, calls=%fused_computation.12 | convolution fusion | flops 404754432 | bytes 1057408 | tf_op jit(solution)/shard_map/dot_general | solution.py:82
  205.2 0.8 fusion.13
  205.9 0.7 copy.21
  (18 shorter events, 0.1 us)
Async XLA Ops:
  7.2 1.0 copy-start
  7.2 63.7 %reduce-scatter.2.cloned.1.call-start = ((), (), s32[]{:S(2)}) async-start(), calls=%async_computation.1 | async-start | bytes 1310720 | tf_op jit(solution)/shard_map/reduce_scatter | solution.py:61
  9.1 28.9 %copy-start.7 = (s32[1,1,1,128]{3,2,1,0:T(1,128)S(1)}, s32[1,1,1,128]{3,2,1,0:T(1,128)}, u32[]{:S(2)}) copy-start(s32[1,1,1,128]{3,2,1,0:T(1,128)} %param.18) | copy-start | bytes 1540
  9.1 7.0 %collective-permute-start = (f32[640,32]{0,1:T(8,128)S(1)}, f32[640,32]{0,1:T(8,128)S(1)}, u32[]{:S(2)}, u32[]{:S(2)}) collective-permute-start(f32[640,32]{0,1:T(8,128)S(1)} %get-tuple-element.145), channel_id=1, source_target_pairs={{0,8},{8,16},{16,24},{1,9},{9,17},{17,25},{2,10},{10,18},{18,26},{... | collective-permute-start | bytes 245768 | tf_op jit(solution)/shard_map/while/body/eval_jaxpr/ppermute | solution.py:10
  19.2 6.3 %collective-permute-start = (f32[640,32]{0,1:T(8,128)S(1)}, f32[640,32]{0,1:T(8,128)S(1)}, u32[]{:S(2)}, u32[]{:S(2)}) collective-permute-start(f32[640,32]{0,1:T(8,128)S(1)} %get-tuple-element.145), channel_id=1, source_target_pairs={{0,8},{8,16},{16,24},{1,9},{9,17},{17,25},{2,10},{10,18},{18,26},{... | collective-permute-start | bytes 245768 | tf_op jit(solution)/shard_map/while/body/eval_jaxpr/ppermute | solution.py:10
  28.6 6.3 %collective-permute-start = (f32[640,32]{0,1:T(8,128)S(1)}, f32[640,32]{0,1:T(8,128)S(1)}, u32[]{:S(2)}, u32[]{:S(2)}) collective-permute-start(f32[640,32]{0,1:T(8,128)S(1)} %get-tuple-element.145), channel_id=1, source_target_pairs={{0,8},{8,16},{16,24},{1,9},{9,17},{17,25},{2,10},{10,18},{18,26},{... | collective-permute-start | bytes 245768 | tf_op jit(solution)/shard_map/while/body/eval_jaxpr/ppermute | solution.py:10
  41.3 61.1 %copy-start.4 = (f32[2048,32]{0,1:T(8,128)S(1)}, f32[2048,32]{0,1:T(8,128)}, u32[]{:S(2)}) copy-start(f32[2048,32]{0,1:T(8,128)} %param.20) | copy-start | bytes 786436
  41.4 57.7 %all-gather.6.cloned.1.call-start = ((), (), s32[]{:S(2)}) async-start(), calls=%async_computation.4 | async-start | bytes 2359296 | tf_op jit(solution)/shard_map/all_gather | solution.py:69
  70.9 113.4 %all-reduce.2.cloned.1.call-start = ((), (), s32[]{:S(2)}) async-start(), calls=%async_computation.2 | async-start | bytes 524288 | tf_op jit(solution)/shard_map/psum | solution.py:78
  102.5 81.9 %copy-start.2 = (bf16[1,1,1,1,256,640]{5,4,3,2,1,0:T(8,128)(2,1)S(1)}, bf16[1,1,1,1,256,640]{5,4,3,2,1,0:T(8,128)(2,1)}, u32[]{:S(2)}) copy-start(bf16[1,1,1,1,256,640]{5,4,3,2,1,0:T(8,128)(2,1)} %param.16) | copy-start | bytes 983044
  102.5 82.1 %copy-start.3 = (bf16[1,1,1,1,256,256]{5,4,3,2,1,0:T(8,128)(2,1)S(1)}, bf16[1,1,1,1,256,256]{5,4,3,2,1,0:T(8,128)(2,1)}, u32[]{:S(2)}) copy-start(bf16[1,1,1,1,256,256]{5,4,3,2,1,0:T(8,128)(2,1)} %param.15) | copy-start | bytes 393220
  102.5 82.1 %copy-start.6 = (bf16[1,1,1,1,256,32]{4,5,3,2,1,0:T(8,128)(2,1)S(1)}, bf16[1,1,1,1,256,32]{4,5,3,2,1,0:T(8,128)(2,1)}, u32[]{:S(2)}) copy-start(bf16[1,1,1,1,256,32]{4,5,3,2,1,0:T(8,128)(2,1)} %param.12) | copy-start | bytes 49156
  113.1 92.0 %copy-start.5 = (bf16[1,1,1,1,256,128]{5,4,3,2,1,0:T(8,128)(2,1)S(1)}, bf16[1,1,1,1,256,128]{5,4,3,2,1,0:T(8,128)(2,1)}, u32[]{:S(2)}) copy-start(bf16[1,1,1,1,256,128]{5,4,3,2,1,0:T(8,128)(2,1)} %param.17) | copy-start | bytes 196612
  113.2 88.5 %all-gather.4.cloned.1.call-start = ((), (), s32[]{:S(2)}) async-start(), calls=%async_computation.3 | async-start | bytes 1310720 | tf_op jit(solution)/shard_map/all_gather | solution.py:79
  184.3 21.6 %copy-start.1 = (f32[2048,32]{0,1:T(8,128)S(1)}, f32[2048,32]{0,1:T(8,128)}, u32[]{:S(2)}) copy-start(f32[2048,32]{0,1:T(8,128)} %all-reduce.2.cloned.1.call-done) | copy-start | bytes 786436
Sparse Core Ops, SparseCore 0:
  41.5 29.3 reduce-scatter.1
  72.8 26.2 all-gather.5
  113.3 71.0 all-reduce.1
  185.7 15.8 all-gather.3
